TPU v7x, 512 devices: a whole 4x4x16 slice. The times are simulated.
512 devices in a mesh: segment: 4 (over x), rep: 8 (over y, core), box: 16 (over z).
Axes of the slice: x: 4, y: 4, z: 16, core: 2. Of those that a mesh axis runs over, the one named last changes fastest.
Arguments:
- centers: float32 [512, 4, 4, 512], P(('rep', 'box')), may hold values from -6 to 6
- box_radii: float32 [512, 4, 4, 512], P(('rep', 'box')), may hold values from 0.001 to 0.01
- labels: int32 [512], P(('rep', 'box')), may hold values from 0 to 9
- certified: int32 [512], P(('rep', 'box')), may hold values from 0 to 1, as said below
- conv_weights: bfloat16 [4, 9, 512, 512], P('segment', None, 'box'), may hold values from -0.01171875 to 0.01171875
- conv_bias: float32 [4, 512], P('segment'), may hold values from -1.2 to 1.2
- head_weight: bfloat16 [512, 10], replicated, may hold values from -0.25 to 0.25
- head_bias: float32 [10], replicated, may hold values from -4 to 4
Outputs:
- lower_bounds: float32 [128, 4, 5], P(('rep', 'box'), 'segment')
Inputs may be any that keep to these rules, and one draw needn't show every extreme that they name: `certified`: for each box index and each i, the devices 2i and 2i + 1 along rep hold 4 boxes with value 0 together; in each box index some such pair has all 4 of them on one device.
All inputs are finite; a program needn't handle non-finite values.
Results may differ from a plain program's by a relative error of at most 0.00055.
Values may be sent and summed in bfloat16 or wider, within the bound.
A program may use at most 64 MiB of HBM per device.

v0:
```python
import jax
import jax.numpy as jnp
from jax import lax
from jax.sharding import PartitionSpec as P

K = 5
MICRO = 2
highest = lax.Precision.HIGHEST


def shifted(x, axis, by):
    count = lax.axis_size(axis)
    pairs = [(i, i + by) for i in range(count) if 0 <= i + by < count]
    return lax.ppermute(x, axis, pairs)


def partner(value, axis, apart):
    mask = 2**apart
    pairs = [(source, source ^ mask) for source in range(lax.axis_size(axis))]
    return lax.ppermute(value, axis, pairs)


def in_blocks(x, dim, count):
    lengths = x.shape
    parts = x.reshape(*lengths[:dim], count, lengths[dim] // count, *lengths[dim + 1 :])
    return jnp.moveaxis(parts, dim, 0)


def summed_on_arrival(x, axis, dim):
    count = lax.axis_size(axis)
    parts = lax.all_to_all(in_blocks(x, dim, count), axis, 0, 0, tiled=True)
    return jnp.sum(parts, axis=0)


def convolve(values, kernel_cols):
    extent = values.shape[1]
    padded = jnp.pad(values, ((0, 0), (1, 1), (1, 1), (0, 0)))
    windows = []
    for tap_index in range(9):
        row_shift, col_shift = divmod(tap_index, 3)
        windows.append(padded[:, row_shift : row_shift + extent, col_shift : col_shift + extent, :])
    stacked = jnp.concatenate(windows, axis=3)
    return lax.dot_general(
        stacked, kernel_cols, (((3,), (0,)), ((), ())), preferred_element_type=jnp.float32
    )


def convolve_back(gradient, kernel_rows):
    extent = gradient.shape[1]
    padded = jnp.pad(gradient, ((0, 0), (1, 1), (1, 1), (0, 0)))
    windows = []
    for tap_index in range(9):
        row_shift, col_shift = divmod(tap_index, 3)
        windows.append(
            padded[
                :, 2 - row_shift : 2 - row_shift + extent, 2 - col_shift : 2 - col_shift + extent, :
            ]
        )
    stacked = jnp.concatenate(windows, axis=3)
    return lax.dot_general(
        stacked, kernel_rows, (((3,), (0,)), ((), ())), preferred_element_type=jnp.float32
    )


def forward_layer(middle, radius, kernel_cols, magnitude_cols, shift_bias):
    centre = convolve(middle.astype(jnp.bfloat16), kernel_cols) + shift_bias
    spread = convolve(radius.astype(jnp.bfloat16), magnitude_cols)
    lower_edge = centre - spread
    upper_edge = centre + spread
    upper_pos = jax.nn.relu(upper_edge)
    lower_neg = jax.nn.relu(-lower_edge)
    lower_pos = jax.nn.relu(lower_edge)
    slope_now = upper_pos / (upper_pos + lower_neg)
    intercept = slope_now * lower_neg
    middle = middle + 0.5 * (upper_pos + lower_pos)
    radius = radius + 0.5 * (upper_pos - lower_pos)
    return (middle, radius, slope_now, intercept)


def backward_layer(coeffs, slope_now, intercept, kernel_rows, shift_bias):
    scaled = coeffs * slope_now[:, None]
    layer_term = jnp.sum(
        scaled * shift_bias + jnp.minimum(coeffs, 0.0) * intercept[:, None], axis=(2, 3, 4)
    )
    gradient = scaled.astype(jnp.bfloat16).reshape((-1,) + scaled.shape[2:])
    coeffs = coeffs + convolve_back(gradient, kernel_rows).reshape(coeffs.shape)
    return (coeffs, layer_term)


def head_coeffs(label_box, head_weight, head_bias, extent, channels):
    classes = head_bias.shape[0]
    spec_rows = jnp.arange(K, dtype=jnp.int32)[None, :]
    others = (label_box[:, None] + 1 + spec_rows) % classes
    class_ids = jnp.arange(classes, dtype=jnp.int32)
    selector = (class_ids[None, None, :] == label_box[:, None, None]).astype(jnp.float32) - (
        class_ids[None, None, :] == others[:, :, None]
    ).astype(jnp.float32)
    pooled = jnp.einsum(
        "bkc,fc->bkf", selector, head_weight.astype(jnp.float32), precision=highest
    ) / float(extent * extent)
    offset = jnp.einsum("bkc,c->bk", selector, head_bias, precision=highest)
    coeffs = jnp.broadcast_to(
        pooled[:, :, None, None, :], (label_box.shape[0], K, extent, extent, channels)
    )
    return (coeffs, offset)


def concretize(coeffs, centre_box, radius_box):
    return jnp.sum(
        coeffs * centre_box[:, None] - jnp.abs(coeffs) * radius_box[:, None], axis=(2, 3, 4)
    )


def run_sections(
    centres,
    radii_in,
    labels_in,
    conv_weights,
    conv_bias,
    head_weight,
    head_bias,
    segment_index,
    segment_count,
):
    rows_total = centres.shape[0]
    micro_rows = rows_total // MICRO
    extent = centres.shape[1]
    channels = centres.shape[3]
    kernel = lax.all_gather(conv_weights, "box", axis=2, tiled=True)[0]
    kernel_cols = jnp.transpose(kernel, (0, 2, 1)).reshape(9 * channels, channels)
    magnitude_cols = jnp.abs(kernel_cols)
    shift_bias = conv_bias[0]
    steps_total = MICRO + segment_count - 1
    at_first = segment_index == 0
    at_last = segment_index == segment_count - 1
    block_shape = (micro_rows, extent, extent, channels)
    slopes = jnp.zeros(centres.shape, jnp.float32)
    intercepts = jnp.zeros(centres.shape, jnp.float32)
    incoming = (jnp.zeros(block_shape, jnp.float32), jnp.zeros(block_shape, jnp.float32))

    def section_forward(operands):
        return forward_layer(operands[0], operands[1], kernel_cols, magnitude_cols, shift_bias)

    def spare_forward(operands):
        return (operands[0], operands[1], jnp.zeros_like(operands[0]), jnp.zeros_like(operands[0]))

    for step_index in range(steps_total):
        micro_index = step_index - segment_index
        active = (micro_index >= 0) & (micro_index < MICRO)
        row_start = jnp.clip(micro_index, 0, MICRO - 1) * micro_rows
        own_middle = lax.dynamic_slice_in_dim(centres, row_start, micro_rows, 0)
        own_radius = lax.dynamic_slice_in_dim(radii_in, row_start, micro_rows, 0)
        middle = jnp.where(at_first, own_middle, incoming[0])
        radius = jnp.where(at_first, own_radius, incoming[1])
        new_middle, new_radius, slope_now, intercept = lax.cond(
            active, section_forward, spare_forward, (middle, radius)
        )
        old_slope = lax.dynamic_slice_in_dim(slopes, row_start, micro_rows, 0)
        old_intercept = lax.dynamic_slice_in_dim(intercepts, row_start, micro_rows, 0)
        slopes = lax.dynamic_update_slice_in_dim(
            slopes, jnp.where(active, slope_now, old_slope), row_start, 0
        )
        intercepts = lax.dynamic_update_slice_in_dim(
            intercepts, jnp.where(active, intercept, old_intercept), row_start, 0
        )
        if step_index < steps_total - 1:
            incoming = (
                shifted(new_middle.astype(jnp.bfloat16), "segment", 1).astype(new_middle.dtype),
                shifted(new_radius.astype(jnp.bfloat16), "segment", 1).astype(new_radius.dtype),
            )
    kernel = lax.all_gather(conv_weights, "box", axis=2, tiled=True)[0]
    kernel_rows = kernel.reshape(9 * channels, channels)

    def section_back(operands):
        coeffs, slope_block, intercept_block, centre_block, radius_block, offset = operands
        new_coeffs, layer_term = backward_layer(
            coeffs, slope_block, intercept_block, kernel_rows, shift_bias
        )
        layer_term = layer_term + jnp.where(at_last, offset, 0.0)
        layer_term = layer_term + jnp.where(
            at_first, concretize(new_coeffs, centre_block, radius_block), 0.0
        )
        return (new_coeffs, layer_term)

    def spare_back(operands):
        return (operands[0], jnp.zeros_like(operands[5]))

    contrib = jnp.zeros((rows_total, K), jnp.float32)
    arriving = jnp.zeros((micro_rows, K, extent, extent, channels), jnp.bfloat16)
    for step_index in range(steps_total):
        micro_index = step_index - (segment_count - 1 - segment_index)
        active = (micro_index >= 0) & (micro_index < MICRO)
        row_start = jnp.clip(micro_index, 0, MICRO - 1) * micro_rows
        label_block = lax.dynamic_slice_in_dim(labels_in, row_start, micro_rows, 0)
        head_part, offset = head_coeffs(label_block, head_weight, head_bias, extent, channels)
        coeffs = jnp.where(at_last, head_part, arriving.astype(jnp.float32))
        operands = (
            coeffs,
            lax.dynamic_slice_in_dim(slopes, row_start, micro_rows, 0),
            lax.dynamic_slice_in_dim(intercepts, row_start, micro_rows, 0),
            lax.dynamic_slice_in_dim(centres, row_start, micro_rows, 0),
            lax.dynamic_slice_in_dim(radii_in, row_start, micro_rows, 0),
            offset,
        )
        new_coeffs, layer_term = lax.cond(active, section_back, spare_back, operands)
        old_term = lax.dynamic_slice_in_dim(contrib, row_start, micro_rows, 0)
        contrib = lax.dynamic_update_slice_in_dim(
            contrib, jnp.where(active, layer_term, old_term), row_start, 0
        )
        if step_index < steps_total - 1:
            arriving = shifted(new_coeffs.astype(jnp.bfloat16), "segment", -1)
    return contrib


def per_device(
    centers, box_radii, labels, certified, conv_weights, conv_bias, head_weight, head_bias
):
    segment_count = lax.axis_size("segment")
    segment_index = lax.axis_index("segment")
    box_count = centers.shape[0]
    alive_rows = 1 - certified
    half_rows = box_count // 2
    tail_shape = centers.shape[1:]
    live_rank = jnp.cumsum(alive_rows) - alive_rows
    own_total = jnp.sum(alive_rows)
    slots = jnp.arange(half_rows, dtype=jnp.int32)
    is_live = alive_rows[None, :] > 0
    keep_map = ((slots[:, None] == live_rank[None, :]) & is_live).astype(jnp.float32)
    send_map = ((slots[:, None] + half_rows == live_rank[None, :]) & is_live).astype(jnp.float32)
    fill_map = (slots[:, None] == own_total + slots[None, :]).astype(jnp.float32)
    flat_centres = centers.reshape(box_count, -1)
    flat_radii = box_radii.reshape(box_count, -1)
    label_tags = (labels + 1).astype(jnp.float32)[:, None]
    got_centres, got_radii, got_tags = partner(
        (
            jnp.dot(send_map, flat_centres, precision=highest),
            jnp.dot(send_map, flat_radii, precision=highest),
            jnp.dot(send_map, label_tags, precision=highest),
        ),
        "rep",
        0,
    )
    work_centres = (
        jnp.dot(keep_map, flat_centres, precision=highest)
        + jnp.dot(fill_map, got_centres, precision=highest)
    ).reshape((half_rows,) + tail_shape)
    work_radii = (
        jnp.dot(keep_map, flat_radii, precision=highest)
        + jnp.dot(fill_map, got_radii, precision=highest)
    ).reshape((half_rows,) + tail_shape)
    work_tags = jnp.dot(keep_map, label_tags, precision=highest) + jnp.dot(
        fill_map, got_tags, precision=highest
    )
    work_labels = jnp.maximum(work_tags[:, 0].astype(jnp.int32) - 1, 0)
    contrib = run_sections(
        work_centres,
        work_radii,
        work_labels,
        conv_weights,
        conv_bias,
        head_weight,
        head_bias,
        segment_index,
        segment_count,
    )
    outgoing = jnp.dot(fill_map.T, contrib, precision=highest)
    returned = partner(outgoing, "rep", 0)
    per_box = jnp.dot(keep_map.T, contrib, precision=highest) + jnp.dot(
        send_map.T, returned, precision=highest
    )
    summed = summed_on_arrival(per_box, "segment", 0)
    return summed[None]


def solution(mesh):
    placed = (
        P(("rep", "box"), None, None, None),
        P(("rep", "box"), None, None, None),
        P(("rep", "box")),
        P(("rep", "box")),
        P("segment", None, "box", None),
        P("segment", None),
        P(),
        P(),
    )
    return jax.shard_map(
        per_device,
        mesh=mesh,
        in_specs=placed,
        out_specs=P(("rep", "box"), "segment", None),
        check_vma=False,
    )
```

profile of v0, /device:TPU:1, one launch (start us, length us, event | category | flops | bytes accessed | tf_op | source)
XLA Modules:
  0.0 220.3 jit_solution(12544865204578964342)
XLA Ops:
  11.4 8.7 %collective-permute-start.1 = (f32[2,8192]{1,0:T(2,128)S(1)}, f32[2,8192]{1,0:T(2,128)S(1)}, u32[]{:S(2)}, u32[]{:S(2)}) collective-permute-start(f32[2,8192]{1,0:T(2,128)S(1)} %fusion.194), channel_id=1, source_target_pairs={{0,16},{16,0},{32,48},{48,32},{64,80},{80,64},{96,112},{112,96},{1... | collective-permute-start | bytes 196616 | tf_op jit(solution)/shard_map/ppermute | solution.py:20
  21.4 1.9 collective-permute-start.2
  23.5 2.4 %collective-permute-start = (f32[2,1]{0,1:T(1,128)S(1)}, f32[2,1]{0,1:T(1,128)S(1)}, u32[]{:S(2)}, u32[]{:S(2)}) collective-permute-start(f32[2,1]{0,1:T(1,128)S(1)} %convolution_bitcast_fusion.1), channel_id=1, source_target_pairs={{0,16},{16,0},{32,48},{48,32},{64,80},{80,64},{96,112},{112,96},{1... | collective-permute-start | bytes 32 | tf_op jit(solution)/shard_map/ppermute | solution.py:20
  37.2 48.1 %all-gather.2.cloned.1.call-done = bf16[1,9,512,512]{3,2,1,0:T(8,128)(2,1)} async-done(((bf16[1,9,32,512]{3,2,1,0:T(8,128)(2,1)}), bf16[1,9,512,512]{3,2,1,0:T(8,128)(2,1)}) %all-gather.2.cloned.1.call-update) | async-done | bytes 4718608 | tf_op jit(solution)/shard_map/all_gather | solution.py:129
  85.3 6.6 %copy.10 = bf16[9,512,512]{2,1,0:T(8,128)(2,1)} copy(bf16[9,512,512]{1,2,0:T(8,128)(2,1)} %bitcast.356) | data formatting | bytes 9437184 | tf_op jit(solution)/shard_map/transpose | solution.py:130
  92.0 5.1 %bitcast_abs_fusion = bf16[4608,512]{1,0:T(8,128)(2,1)} fusion(bf16[9,512,512]{2,1,0:T(8,128)(2,1)} %copy.10), kind=kLoop, calls=%fused_computation.517 | loop fusion | flops 2359296 | bytes 9437184 | tf_op jit(solution)/shard_map/abs | solution.py:131
  97.1 4.5 %conditional.10 = (f32[1,4,4,512]{3,2,1,0:T(4,128)S(1)}, f32[1,4,4,512]{3,2,1,0:T(4,128)S(1)}, f32[1,4,4,512]{3,2,1,0:T(4,128)S(1)}, f32[1,4,4,512]{3,2,1,0:T(4,128)S(1)}) conditional(s32[]{:T(128)} %convert_element_type.272, (f32[1,4,4,512]{3,2,1,0:T(4,128)S(1)}, f32[1,4,4,512]{3,2,1,0:T(4,128)S(1)}) %tuple.108, (f32[1,4,4,512]{3,2,1,0:T(4,128)S(1)}, ...), branch_computations={%region_2.3_spmd, %region_3.4_spmd} | conditional | flops 151175168 | bytes 10913824 | solution.py:155
  97.3 3.1 %fusion = f32[4,4,512]{2,1,0:T(4,128)S(1)} fusion(bf16[4608,512]{1,0:T(8,128)(2,1)} %get-tuple-element.592, bf16[1,4,4,4608]{3,2,1,0:T(4,128)(2,1)S(1)} %constant_dynamic-update-slice_fusion.9), kind=kOutput, calls=%fused_computation | convolution fusion | flops 75497472 | bytes 4898816 | tf_op jit(solution)/shard_map/cond/branch_1_fun/dot_general | solution.py:43
  105.1 4.9 %conditional.11 = (f32[1,4,4,512]{3,2,1,0:T(4,128)S(1)}, f32[1,4,4,512]{3,2,1,0:T(4,128)S(1)}, f32[1,4,4,512]{3,2,1,0:T(4,128)S(1)}, f32[1,4,4,512]{3,2,1,0:T(4,128)S(1)}) conditional(s32[]{:T(128)} %convert_element_type.273, (f32[1,4,4,512]{3,2,1,0:T(4,128)S(1)}, f32[1,4,4,512]{3,2,1,0:T(4,128)S(1)}) %tuple.110, (f32[1,4,4,512]{3,2,1,0:T(4,128)S(1)}, ...), branch_computations={%region_4.5_spmd, %region_5.6_spmd} | conditional | flops 151175168 | bytes 29788220 | solution.py:155
  105.3 3.3 %fusion.9 = f32[4,4,512]{2,1,0:T(4,128)S(1)} fusion(bf16[4608,512]{1,0:T(8,128)(2,1)} %get-tuple-element.599, bf16[1,4,4,4608]{3,2,1,0:T(4,128)(2,1)S(1)} %constant_dynamic-update-slice_fusion.27), kind=kOutput, calls=%fused_computation.47 | convolution fusion | flops 75497472 | bytes 4898816 | tf_op jit(solution)/shard_map/cond/branch_1_fun/dot_general | solution.py:43
  110.0 3.6 %collective-permute-start.6 = (bf16[1,4,4,512]{3,2,1,0:T(4,128)(2,1)S(1)}, bf16[1,4,4,512]{3,2,1,0:T(4,128)(2,1)S(1)}, u32[]{:S(2)}, u32[]{:S(2)}) collective-permute-start(bf16[1,4,4,512]{3,2,1,0:T(4,128)(2,1)S(1)} %convert_element_type.281), channel_id=1, source_target_pairs={{0,128},{128,256},{256,384},{1,129},{129,257},{257,385},{2,130},{1... | collective-permute-start | bytes 49160 | tf_op jit(solution)/shard_map/ppermute | solution.py:14
  116.5 8.5 %collective-permute-start.8 = (bf16[1,4,4,512]{3,2,1,0:T(4,128)(2,1)S(1)}, bf16[1,4,4,512]{3,2,1,0:T(4,128)(2,1)S(1)}, u32[]{:S(2)}, u32[]{:S(2)}) collective-permute-start(bf16[1,4,4,512]{3,2,1,0:T(4,128)(2,1)S(1)} %convert_element_type.286), channel_id=1, source_target_pairs={{0,128},{128,256},{256,384},{1,129},{129,257},{257,385},{2,130},{1... | collective-permute-start | bytes 49160 | tf_op jit(solution)/shard_map/ppermute | solution.py:14
  127.9 3.6 %collective-permute-start.10 = (bf16[1,4,4,512]{3,2,1,0:T(4,128)(2,1)S(1)}, bf16[1,4,4,512]{3,2,1,0:T(4,128)(2,1)S(1)}, u32[]{:S(2)}, u32[]{:S(2)}) collective-permute-start(bf16[1,4,4,512]{3,2,1,0:T(4,128)(2,1)S(1)} %convert_element_type.291), channel_id=1, source_target_pairs={{0,128},{128,256},{256,384},{1,129},{129,257},{257,385},{2,130},{1... | collective-permute-start | bytes 49160 | tf_op jit(solution)/shard_map/ppermute | solution.py:14
  131.5 6.8 %collective-permute-start.9 = (bf16[1,4,4,512]{3,2,1,0:T(4,128)(2,1)S(1)}, bf16[1,4,4,512]{3,2,1,0:T(4,128)(2,1)S(1)}, u32[]{:S(2)}, u32[]{:S(2)}) collective-permute-start(bf16[1,4,4,512]{3,2,1,0:T(4,128)(2,1)S(1)} %convert_element_type.289), channel_id=1, source_target_pairs={{0,128},{128,256},{256,384},{1,129},{129,257},{257,385},{2,130},{1... | collective-permute-start | bytes 49160 | tf_op jit(solution)/shard_map/ppermute | solution.py:14
  140.9 4.6 %collective-permute-done.11 = bf16[1,5,4,4,512]{4,1,3,2,0:T(8,128)(2,1)S(1)} collective-permute-done((bf16[1,5,4,4,512]{4,1,3,2,0:T(8,128)(2,1)S(1)}, bf16[1,5,4,4,512]{4,1,3,2,0:T(8,128)(2,1)S(1)}, u32[]{:S(2)}, u32[]{:S(2)}) %collective-permute-start.11) | collective-permute-done | bytes 81952 | tf_op jit(solution)/shard_map/ppermute | solution.py:14
  146.9 4.6 %collective-permute-done.12 = bf16[1,5,4,4,512]{4,1,3,2,0:T(8,128)(2,1)S(1)} collective-permute-done((bf16[1,5,4,4,512]{4,1,3,2,0:T(8,128)(2,1)S(1)}, bf16[1,5,4,4,512]{4,1,3,2,0:T(8,128)(2,1)S(1)}, u32[]{:S(2)}, u32[]{:S(2)}) %collective-permute-start.12) | collective-permute-done | bytes 81952 | tf_op jit(solution)/shard_map/ppermute | solution.py:14
  153.0 18.7 %collective-permute-done.13 = bf16[1,5,4,4,512]{4,1,3,2,0:T(8,128)(2,1)S(1)} collective-permute-done((bf16[1,5,4,4,512]{4,1,3,2,0:T(8,128)(2,1)S(1)}, bf16[1,5,4,4,512]{4,1,3,2,0:T(8,128)(2,1)S(1)}, u32[]{:S(2)}, u32[]{:S(2)}) %collective-permute-start.13) | collective-permute-done | bytes 81952 | tf_op jit(solution)/shard_map/ppermute | solution.py:14
  171.7 4.4 %conditional.18 = (f32[1,5,4,4,512]{4,1,3,2,0:T(8,128)S(1)}, f32[1,5]{1,0:T(1,128)S(1)}) conditional(s32[]{:T(128)} %convert_element_type.303, f32[1,5,4,4,512]{4,1,3,2,0:T(8,128)S(1)} %convert_select_fusion, (f32[2,4,4,512]{3,2,1,0:T(4,128)S(1)}, s32[]{:T(128)}, f32[1,5,4,4,512]{4,1,3,2,0:T(8,128)S(1)}, bf16[4608,512]{1,0:T(8,128)(2,1)}, ...), branch_computations={%region_24.25_spmd, %region_25.28_spmd} | conditional | flops 378019872 | bytes 8734866 | solution.py:205
  172.2 3.9 %subtract_reduce_fusion.3 = (f32[5]{0:T(128)S(1)}, f32[1,5,4,4,512]{4,1,3,2,0:T(8,128)S(1)}) fusion(f32[4,4,512]{2,1,0:T(4,128)S(1)} %get-tuple-element.776, f32[4,4,512]{2,1,0:T(4,128)S(1)} %get-tuple-element.777, f32[1,5,4,4,512]{4,1,3,2,0:T(8,128)S(1)} %get-tuple-element.656, bf16[5,4,4,4608]{3,0,2,1:T(8,128)(2,1)S(1)} %fusion.122, ...), kind=kOutput, calls=%fused_computation.349 | convolution fusion | flops 377733120 | bytes 5849108 | tf_op jit(solution)/shard_map/cond/branch_1_fun/dot_general | solution.py:60
  177.5 4.4 %collective-permute-done.14 = bf16[1,5,4,4,512]{4,1,3,2,0:T(8,128)(2,1)S(1)} collective-permute-done((bf16[1,5,4,4,512]{4,1,3,2,0:T(8,128)(2,1)S(1)}, bf16[1,5,4,4,512]{4,1,3,2,0:T(8,128)(2,1)S(1)}, u32[]{:S(2)}, u32[]{:S(2)}) %collective-permute-start.14) | collective-permute-done | bytes 81952 | tf_op jit(solution)/shard_map/ppermute | solution.py:14
  182.0 4.4 %conditional.19 = (f32[1,5]{1,0:T(1,128)S(1)}) conditional(s32[]{:T(128)} %convert_element_type.308, () %tuple.122, (f32[5,512]{1,0:T(8,128)S(1)}, pred[1,5,4,4,512]{4,1,3,2,0:T(8,128)(4,1)S(1)}, f32[1,5,4,4,512]{4,1,3,2,0:T(8,128)S(1)}, f32[2,4,4,512]{3,2,1,0:T(4,128)S(1)}, s32[]{:T(128)}, /*index=5*/f32[1,512]{1,0:T(1,128)S(1)}, ...), branch_computations={%region_28.29_spmd, %region_29.32_spmd} | conditional | flops 378104352 | bytes 8693898 | solution.py:205
  182.5 3.9 %subtract_reduce_fusion.4 = f32[5]{0:T(128)S(1)} fusion(bf16[5,4,4,4608]{3,0,2,1:T(8,128)(2,1)S(1)} %fusion.144, bf16[4608,512]{1,0:T(8,128)(2,1)} %get-tuple-element.677, f32[4,4,512]{2,1,0:T(4,128)S(1)} %get-tuple-element.782, f32[4,4,512]{2,1,0:T(4,128)S(1)} %get-tuple-element.783, pred[1,5,4,4,512]{4,1,3,2,0:T(8,128)(4,1)S(1)} %get-tuple-element.667, ...), kind=kOutput, calls=%fused_computation.383 | convolution fusion | flops 377774080 | bytes 5736468 | tf_op jit(solution)/shard_map/cond/branch_1_fun/dot_general | solution.py:60
  186.8 18.7 %collective-permute-start.15 = (f32[2,5]{1,0:T(2,128)S(1)}, f32[2,5]{1,0:T(2,128)S(1)}, u32[]{:S(2)}, u32[]{:S(2)}) collective-permute-start(f32[2,5]{1,0:T(2,128)S(1)} %fusion.174), channel_id=1, source_target_pairs={{0,16},{16,0},{32,48},{48,32},{64,80},{80,64},{96,112},{112,96},{1... | collective-permute-start | bytes 128 | tf_op jit(solution)/shard_map/ppermute | solution.py:20
  206.5 6.5 %all_to_all.5 = f32[4,1,5]{2,1,0:T(1,128)S(1)} all-to-all(f32[4,1,5]{2,1,0:T(1,128)S(1)} %bitcast.376), channel_id=1, replica_groups=mesh['segment'=4,'rep'=8,'box'=16] {'segment'}, dimensions={0} | all-to-all | bytes 160 | tf_op jit(solution)/shard_map/all_to_all | solution.py:31
  (215 shorter events, 35.6 us)
Async XLA Ops:
  6.5 28.8 %copy-start = (bf16[512,10]{0,1:T(8,128)(2,1)S(1)}, bf16[512,10]{0,1:T(8,128)(2,1)}, u32[]{:S(2)}) copy-start(bf16[512,10]{0,1:T(8,128)(2,1)} %param.34) | copy-start | bytes 30724
  6.5 16.8 %copy-start.7 = (s32[4]{0:T(128)S(1)}, s32[4]{0:T(128)}, u32[]{:S(2)}) copy-start(s32[4]{0:T(128)} %param.30) | copy-start | bytes 52
  6.5 27.9 %copy-start.8 = (f32[10]{0:T(128)S(1)}, f32[10]{0:T(128)}, u32[]{:S(2)}) copy-start(f32[10]{0:T(128)} %param.35) | copy-start | bytes 124
  6.5 78.8 %all-gather.2.cloned.1.call-start = ((), (), s32[]{:S(2)}) async-start(), calls=%async_computation.1 | async-start | bytes 5013504 | tf_op jit(solution)/shard_map/all_gather | solution.py:129
  11.4 25.1 %collective-permute-start.1 = (f32[2,8192]{1,0:T(2,128)S(1)}, f32[2,8192]{1,0:T(2,128)S(1)}, u32[]{:S(2)}, u32[]{:S(2)}) collective-permute-start(f32[2,8192]{1,0:T(2,128)S(1)} %fusion.194), channel_id=1, source_target_pairs={{0,16},{16,0},{32,48},{48,32},{64,80},{80,64},{96,112},{112,96},{1... | collective-permute-start | bytes 196616 | tf_op jit(solution)/shard_map/ppermute | solution.py:20
  21.4 15.4 %collective-permute-start.2 = (f32[2,8192]{1,0:T(2,128)S(1)}, f32[2,8192]{1,0:T(2,128)S(1)}, u32[]{:S(2)}, u32[]{:S(2)}) collective-permute-start(f32[2,8192]{1,0:T(2,128)S(1)} %fusion.196), channel_id=1, source_target_pairs={{0,16},{16,0},{32,48},{48,32},{64,80},{80,64},{96,112},{112,96},{1... | collective-permute-start | bytes 196616 | tf_op jit(solution)/shard_map/ppermute | solution.py:20
  23.5 3.8 %collective-permute-start = (f32[2,1]{0,1:T(1,128)S(1)}, f32[2,1]{0,1:T(1,128)S(1)}, u32[]{:S(2)}, u32[]{:S(2)}) collective-permute-start(f32[2,1]{0,1:T(1,128)S(1)} %convolution_bitcast_fusion.1), channel_id=1, source_target_pairs={{0,16},{16,0},{32,48},{48,32},{64,80},{80,64},{96,112},{112,96},{1... | collective-permute-start | bytes 32 | tf_op jit(solution)/shard_map/ppermute | solution.py:20
  92.0 5.1 %copy-start.1 = (bf16[9,512,512]{2,1,0:T(8,128)(2,1)S(1)}, bf16[9,512,512]{2,1,0:T(8,128)(2,1)}, u32[]{:S(2)}) copy-start(bf16[9,512,512]{2,1,0:T(8,128)(2,1)} %copy.10) | copy-start | bytes 14155780
  92.0 5.1 %copy-start.6 = (f32[1,512]{1,0:T(1,128)S(1)}, f32[1,512]{1,0:T(1,128)}, u32[]{:S(2)}) copy-start(f32[1,512]{1,0:T(1,128)} %param.33) | copy-start | bytes 6148
  101.6 2.7 %collective-permute-start.4 = (bf16[1,4,4,512]{3,2,1,0:T(4,128)(2,1)S(1)}, bf16[1,4,4,512]{3,2,1,0:T(4,128)(2,1)S(1)}, u32[]{:S(2)}, u32[]{:S(2)}) collective-permute-start(bf16[1,4,4,512]{3,2,1,0:T(4,128)(2,1)S(1)} %convert_element_type.276), channel_id=1, source_target_pairs={{0,128},{128,256},{256,384},{1,129},{129,257},{257,385},{2,130},{1... | collective-permute-start | bytes 49160 | tf_op jit(solution)/shard_map/ppermute | solution.py:14
  102.9 2.1 collective-permute-start.3
  105.3 3.8 %copy-start.2 = (bf16[4608,512]{1,0:T(8,128)(2,1)S(1)}, bf16[4608,512]{1,0:T(8,128)(2,1)}, u32[]{:S(2)}) copy-start(bf16[4608,512]{1,0:T(8,128)(2,1)} %get-tuple-element.596) | copy-start | bytes 14155780 | tf_op jit(solution)/shard_map/cond
  110.0 5.6 %collective-permute-start.6 = (bf16[1,4,4,512]{3,2,1,0:T(4,128)(2,1)S(1)}, bf16[1,4,4,512]{3,2,1,0:T(4,128)(2,1)S(1)}, u32[]{:S(2)}, u32[]{:S(2)}) collective-permute-start(bf16[1,4,4,512]{3,2,1,0:T(4,128)(2,1)S(1)} %convert_element_type.281), channel_id=1, source_target_pairs={{0,128},{128,256},{256,384},{1,129},{129,257},{257,385},{2,130},{1... | collective-permute-start | bytes 49160 | tf_op jit(solution)/shard_map/ppermute | solution.py:14
  113.6 2.8 %collective-permute-start.5 = (bf16[1,4,4,512]{3,2,1,0:T(4,128)(2,1)S(1)}, bf16[1,4,4,512]{3,2,1,0:T(4,128)(2,1)S(1)}, u32[]{:S(2)}, u32[]{:S(2)}) collective-permute-start(bf16[1,4,4,512]{3,2,1,0:T(4,128)(2,1)S(1)} %convert_element_type.279), channel_id=1, source_target_pairs={{0,128},{128,256},{256,384},{1,129},{129,257},{257,385},{2,130},{1... | collective-permute-start | bytes 49160 | tf_op jit(solution)/shard_map/ppermute | solution.py:14
  116.5 10.5 %collective-permute-start.8 = (bf16[1,4,4,512]{3,2,1,0:T(4,128)(2,1)S(1)}, bf16[1,4,4,512]{3,2,1,0:T(4,128)(2,1)S(1)}, u32[]{:S(2)}, u32[]{:S(2)}) collective-permute-start(bf16[1,4,4,512]{3,2,1,0:T(4,128)(2,1)S(1)} %convert_element_type.286), channel_id=1, source_target_pairs={{0,128},{128,256},{256,384},{1,129},{129,257},{257,385},{2,130},{1... | collective-permute-start | bytes 49160 | tf_op jit(solution)/shard_map/ppermute | solution.py:14
  125.0 2.8 %collective-permute-start.7 = (bf16[1,4,4,512]{3,2,1,0:T(4,128)(2,1)S(1)}, bf16[1,4,4,512]{3,2,1,0:T(4,128)(2,1)S(1)}, u32[]{:S(2)}, u32[]{:S(2)}) collective-permute-start(bf16[1,4,4,512]{3,2,1,0:T(4,128)(2,1)S(1)} %convert_element_type.284), channel_id=1, source_target_pairs={{0,128},{128,256},{256,384},{1,129},{129,257},{257,385},{2,130},{1... | collective-permute-start | bytes 49160 | tf_op jit(solution)/shard_map/ppermute | solution.py:14
  127.9 10.5 %collective-permute-start.10 = (bf16[1,4,4,512]{3,2,1,0:T(4,128)(2,1)S(1)}, bf16[1,4,4,512]{3,2,1,0:T(4,128)(2,1)S(1)}, u32[]{:S(2)}, u32[]{:S(2)}) collective-permute-start(bf16[1,4,4,512]{3,2,1,0:T(4,128)(2,1)S(1)} %convert_element_type.291), channel_id=1, source_target_pairs={{0,128},{128,256},{256,384},{1,129},{129,257},{257,385},{2,130},{1... | collective-permute-start | bytes 49160 | tf_op jit(solution)/shard_map/ppermute | solution.py:14
  131.5 7.6 %collective-permute-start.9 = (bf16[1,4,4,512]{3,2,1,0:T(4,128)(2,1)S(1)}, bf16[1,4,4,512]{3,2,1,0:T(4,128)(2,1)S(1)}, u32[]{:S(2)}, u32[]{:S(2)}) collective-permute-start(bf16[1,4,4,512]{3,2,1,0:T(4,128)(2,1)S(1)} %convert_element_type.289), channel_id=1, source_target_pairs={{0,128},{128,256},{256,384},{1,129},{129,257},{257,385},{2,130},{1... | collective-permute-start | bytes 49160 | tf_op jit(solution)/shard_map/ppermute | solution.py:14
  139.5 6.0 %collective-permute-start.11 = (bf16[1,5,4,4,512]{4,1,3,2,0:T(8,128)(2,1)S(1)}, bf16[1,5,4,4,512]{4,1,3,2,0:T(8,128)(2,1)S(1)}, u32[]{:S(2)}, u32[]{:S(2)}) collective-permute-start(bf16[1,5,4,4,512]{4,1,3,2,0:T(8,128)(2,1)S(1)} %convert_element_type.296), channel_id=1, source_target_pairs={{128,0},{256,128},{384,256},{129,1},{257,129},{385,257},{130,2},{2... | collective-permute-start | bytes 245768 | tf_op jit(solution)/shard_map/ppermute | solution.py:14
  145.6 6.0 %collective-permute-start.12 = (bf16[1,5,4,4,512]{4,1,3,2,0:T(8,128)(2,1)S(1)}, bf16[1,5,4,4,512]{4,1,3,2,0:T(8,128)(2,1)S(1)}, u32[]{:S(2)}, u32[]{:S(2)}) collective-permute-start(bf16[1,5,4,4,512]{4,1,3,2,0:T(8,128)(2,1)S(1)} %convert_element_type.301), channel_id=1, source_target_pairs={{128,0},{256,128},{384,256},{129,1},{257,129},{385,257},{130,2},{2... | collective-permute-start | bytes 245768 | tf_op jit(solution)/shard_map/ppermute | solution.py:14
  151.7 20.0 %collective-permute-start.13 = (bf16[1,5,4,4,512]{4,1,3,2,0:T(8,128)(2,1)S(1)}, bf16[1,5,4,4,512]{4,1,3,2,0:T(8,128)(2,1)S(1)}, u32[]{:S(2)}, u32[]{:S(2)}) collective-permute-start(bf16[1,5,4,4,512]{4,1,3,2,0:T(8,128)(2,1)S(1)} %convert_element_type.306), channel_id=1, source_target_pairs={{128,0},{256,128},{384,256},{129,1},{257,129},{385,257},{130,2},{2... | collective-permute-start | bytes 245768 | tf_op jit(solution)/shard_map/ppermute | solution.py:14
  176.2 5.7 %collective-permute-start.14 = (bf16[1,5,4,4,512]{4,1,3,2,0:T(8,128)(2,1)S(1)}, bf16[1,5,4,4,512]{4,1,3,2,0:T(8,128)(2,1)S(1)}, u32[]{:S(2)}, u32[]{:S(2)}) collective-permute-start(bf16[1,5,4,4,512]{4,1,3,2,0:T(8,128)(2,1)S(1)} %convert_element_type.311), channel_id=1, source_target_pairs={{128,0},{256,128},{384,256},{129,1},{257,129},{385,257},{130,2},{2... | collective-permute-start | bytes 245768 | tf_op jit(solution)/shard_map/ppermute | solution.py:14
  186.8 19.5 %collective-permute-start.15 = (f32[2,5]{1,0:T(2,128)S(1)}, f32[2,5]{1,0:T(2,128)S(1)}, u32[]{:S(2)}, u32[]{:S(2)}) collective-permute-start(f32[2,5]{1,0:T(2,128)S(1)} %fusion.174), channel_id=1, source_target_pairs={{0,16},{16,0},{32,48},{48,32},{64,80},{80,64},{96,112},{112,96},{1... | collective-permute-start | bytes 128 | tf_op jit(solution)/shard_map/ppermute | solution.py:20
Sparse Core Ops, SparseCore 0:
  9.4 75.8 all-gather.1
where the time goes:
time: 221 us; the launch traced here: 220 us
  waiting for transfers between devices  85 us (38%)
  starting transfers between devices  65.8 us (30%)
  matrix products  20.2 us (9%)
  between operations  17.3 us (8%)
  other arithmetic  13.7 us (6%)
  local copies, waits for them, and re-layouts  11.1 us (5%)
  blocking collectives  6.47 us (3%)
    all_gather x1, waiting for transfers between devices, run_sections(): kernel = lax.all_gather(conv_weights, 'box', axis=2, tiled=True)[0]  48.1 us
    ppermute x12, waiting for transfers between devices, shifted(): return lax.ppermute(x, axis, pairs)  35.3 us
    ppermute x12, starting transfers between devices, shifted(): return lax.ppermute(x, axis, pairs)  34.1 us
    ppermute x4, starting transfers between devices, partner(): return lax.ppermute(value, axis, pairs)  31.7 us
    dot_general x4, matrix products, convolve(): lax.dot_general(stacked, kernel_cols, (((3,), (0,)), ((), ())), preferred...  7.97 us
    dot_general x2, matrix products, convolve_back(): lax.dot_general(stacked, kernel_rows, (((3,), (0,)), ((), ())), preferred...  7.83 us
    transpose x1, local copies, waits for them, and re-layouts, run_sections(): jnp.transpose(kernel, (0, 2, 1)).reshape(9 * channels, channels)  6.65 us
    all_to_all x1, blocking collectives, summed_on_arrival(): parts = lax.all_to_all(in_blocks(x, dim, count), axis, 0, 0, tiled=True)  6.47 us
  transfers between devices with their start and end apart: 17, of which 10 were waited for; matrix products, arithmetic and copies ran while one was open for 6% of the time, Pallas kernels for 0%

commit v1 on v0

--- a/solution.py
+++ b/solution.py
@@ -6,6 +6,12 @@
 K = 5
 MICRO = 2
 highest = lax.Precision.HIGHEST
+sheets_state = lambda content: jnp.concatenate(
+    lax.all_to_all(
+        jnp.stack(lax.axis_size("box") * [content]), axis_name="box", split_axis=0, concat_axis=0
+    ),
+    axis=2,
+)
 
 
 def shifted(x, axis, by):
@@ -126,7 +132,7 @@
     micro_rows = rows_total // MICRO
     extent = centres.shape[1]
     channels = centres.shape[3]
-    kernel = lax.all_gather(conv_weights, "box", axis=2, tiled=True)[0]
+    kernel = sheets_state(conv_weights)[0]
     kernel_cols = jnp.transpose(kernel, (0, 2, 1)).reshape(9 * channels, channels)
     magnitude_cols = jnp.abs(kernel_cols)
     shift_bias = conv_bias[0]

time: 221 us -> 409 us (1.85)
  waiting for transfers between devices: 85 us -> 262 us
  local copies, waits for them, and re-layouts: 11.1 us -> 18.5 us
  starting transfers between devices: 65.8 us -> 70.4 us
    all_to_all x0 -> x1, waiting for transfers between devices: none -> 225 us  [lax.all_to_all(jnp.stack(lax.axis_size('box') * [content]), axis_name='bo...]
    all_gather x1, waiting for transfers between devices: 48.1 us -> 0.02 us  [run_sections(): kernel = lax.all_gather(conv_weights, 'box', axis=2, tiled=True)[0]]
    all_to_all x0 -> x1, starting transfers between devices: none -> 15.9 us  [lax.all_to_all(jnp.stack(lax.axis_size('box') * [content]), axis_name='bo...]
    ppermute x4, starting transfers between devices: 31.7 us -> 20.4 us  [partner(): return lax.ppermute(value, axis, pairs)]
    all_to_all x0 -> x1, local copies, waits for them, and re-layouts: none -> 5.33 us  [lax.all_to_all(jnp.stack(lax.axis_size('box') * [content]), axis_name='bo...]
  transfers between devices with their start and end apart: 17 -> 18, of which waited for: 10 -> 10; matrix products, arithmetic and copies ran while one was open for 6% -> 9% of each run, Pallas kernels for 0% -> 0%
where the time goes in v1:
time: 409 us; the launch traced here: 408 us
  waiting for transfers between devices  262 us (64%)
  starting transfers between devices  70.4 us (17%)
  matrix products  20.2 us (5%)
  local copies, waits for them, and re-layouts  18.5 us (5%)
  between operations  17.4 us (4%)
  other arithmetic  11.8 us (3%)
  blocking collectives  6.47 us (2%)
    all_to_all x1, waiting for transfers between devices, lax.all_to_all(jnp.stack(lax.axis_size('box') * [content]), axis_name='bo...  225 us
    ppermute x12, waiting for transfers between devices, shifted(): return lax.ppermute(x, axis, pairs)  35.8 us
    ppermute x12, starting transfers between devices, shifted(): return lax.ppermute(x, axis, pairs)  34.1 us
    ppermute x4, starting transfers between devices, partner(): return lax.ppermute(value, axis, pairs)  20.4 us
    all_to_all x1, starting transfers between devices, lax.all_to_all(jnp.stack(lax.axis_size('box') * [content]), axis_name='bo...  15.9 us
  transfers between devices with their start and end apart: 18, of which 10 were waited for; matrix products, arithmetic and copies ran while one was open for 9% of the time, Pallas kernels for 0%

profile of v1, /device:TPU:1, one launch (start us, length us, event | category | flops | bytes accessed | tf_op | source)
XLA Modules:
  0.0 407.5 jit_solution(8920458082049388918)
XLA Ops:
  6.5 3.8 stack.2
  10.3 15.9 %all-to-all-start = ((bf16[16,1,9,32,512]{4,3,2,1,0:T(8,128)(2,1)}), bf16[16,1,9,32,512]{4,3,2,1,0:T(8,128)(2,1)}, u32[]{:S(2)}, u32[]{:S(2)}) async-start(bf16[16,1,9,32,512]{4,3,2,1,0:T(8,128)(2,1)} %stack.2), calls=%async_computation | async-start | bytes 9437184 | tf_op jit(solution)/shard_map/all_to_all | solution.py:10
  47.5 224.7 %all-to-all-done = bf16[16,1,9,32,512]{4,3,2,1,0:T(8,128)(2,1)} async-done(((bf16[16,1,9,32,512]{4,3,2,1,0:T(8,128)(2,1)}), bf16[16,1,9,32,512]{4,3,2,1,0:T(8,128)(2,1)}, u32[]{:S(2)}, u32[]{:S(2)}) %all-to-all-start) | async-done | bytes 4718624 | tf_op jit(solution)/shard_map/all_to_all | solution.py:10
  272.1 5.3 %copy.11 = bf16[16,1,9,32,512]{4,3,0,2,1:T(8,128)(2,1)} copy(bf16[16,1,9,32,512]{4,3,2,1,0:T(8,128)(2,1)} %all-to-all-done) | data formatting | bytes 9437184 | tf_op jit(solution)/shard_map/all_to_all | solution.py:10
  277.5 6.7 %copy.12 = bf16[9,512,512]{2,1,0:T(8,128)(2,1)} copy(bf16[9,512,512]{1,2,0:T(8,128)(2,1)} %bitcast.364) | data formatting | bytes 9437184 | tf_op jit(solution)/shard_map/transpose | solution.py:136
  284.1 5.1 %bitcast_abs_fusion = bf16[4608,512]{1,0:T(8,128)(2,1)} fusion(bf16[9,512,512]{2,1,0:T(8,128)(2,1)} %copy.12), kind=kLoop, calls=%fused_computation.517 | loop fusion | flops 2359296 | bytes 9437184 | tf_op jit(solution)/shard_map/abs | solution.py:137
  289.3 4.5 %conditional.10 = (f32[1,4,4,512]{3,2,1,0:T(4,128)S(1)}, f32[1,4,4,512]{3,2,1,0:T(4,128)S(1)}, f32[1,4,4,512]{3,2,1,0:T(4,128)S(1)}, f32[1,4,4,512]{3,2,1,0:T(4,128)S(1)}) conditional(s32[]{:T(128)} %convert_element_type.272, (f32[1,4,4,512]{3,2,1,0:T(4,128)S(1)}, f32[1,4,4,512]{3,2,1,0:T(4,128)S(1)}) %tuple.108, (f32[1,4,4,512]{3,2,1,0:T(4,128)S(1)}, ...), branch_computations={%region_2.3_spmd, %region_3.4_spmd} | conditional | flops 151175168 | bytes 10913824 | solution.py:161
  289.5 3.1 fusion
  297.2 4.9 %conditional.11 = (f32[1,4,4,512]{3,2,1,0:T(4,128)S(1)}, f32[1,4,4,512]{3,2,1,0:T(4,128)S(1)}, f32[1,4,4,512]{3,2,1,0:T(4,128)S(1)}, f32[1,4,4,512]{3,2,1,0:T(4,128)S(1)}) conditional(s32[]{:T(128)} %convert_element_type.273, (f32[1,4,4,512]{3,2,1,0:T(4,128)S(1)}, f32[1,4,4,512]{3,2,1,0:T(4,128)S(1)}) %tuple.110, (f32[1,4,4,512]{3,2,1,0:T(4,128)S(1)}, ...), branch_computations={%region_4.5_spmd, %region_5.6_spmd} | conditional | flops 151175168 | bytes 29788220 | solution.py:161
  297.5 3.3 fusion.9
  302.1 3.6 collective-permute-start.6
  308.7 8.5 %collective-permute-start.8 = (bf16[1,4,4,512]{3,2,1,0:T(4,128)(2,1)S(1)}, bf16[1,4,4,512]{3,2,1,0:T(4,128)(2,1)S(1)}, u32[]{:S(2)}, u32[]{:S(2)}) collective-permute-start(bf16[1,4,4,512]{3,2,1,0:T(4,128)(2,1)S(1)} %convert_element_type.286), channel_id=1, source_target_pairs={{0,128},{128,256},{256,384},{1,129},{129,257},{257,385},{2,130},{1... | collective-permute-start | bytes 49160 | tf_op jit(solution)/shard_map/ppermute | solution.py:20
  320.2 3.6 collective-permute-start.10
  323.9 6.8 %collective-permute-start.9 = (bf16[1,4,4,512]{3,2,1,0:T(4,128)(2,1)S(1)}, bf16[1,4,4,512]{3,2,1,0:T(4,128)(2,1)S(1)}, u32[]{:S(2)}, u32[]{:S(2)}) collective-permute-start(bf16[1,4,4,512]{3,2,1,0:T(4,128)(2,1)S(1)} %convert_element_type.289), channel_id=1, source_target_pairs={{0,128},{128,256},{256,384},{1,129},{129,257},{257,385},{2,130},{1... | collective-permute-start | bytes 49160 | tf_op jit(solution)/shard_map/ppermute | solution.py:20
  333.1 4.6 %collective-permute-done.11 = bf16[1,5,4,4,512]{4,1,3,2,0:T(8,128)(2,1)S(1)} collective-permute-done((bf16[1,5,4,4,512]{4,1,3,2,0:T(8,128)(2,1)S(1)}, bf16[1,5,4,4,512]{4,1,3,2,0:T(8,128)(2,1)S(1)}, u32[]{:S(2)}, u32[]{:S(2)}) %collective-permute-start.11) | collective-permute-done | bytes 81952 | tf_op jit(solution)/shard_map/ppermute | solution.py:20
  339.1 4.4 %collective-permute-done.12 = bf16[1,5,4,4,512]{4,1,3,2,0:T(8,128)(2,1)S(1)} collective-permute-done((bf16[1,5,4,4,512]{4,1,3,2,0:T(8,128)(2,1)S(1)}, bf16[1,5,4,4,512]{4,1,3,2,0:T(8,128)(2,1)S(1)}, u32[]{:S(2)}, u32[]{:S(2)}) %collective-permute-start.12) | collective-permute-done | bytes 81952 | tf_op jit(solution)/shard_map/ppermute | solution.py:20
  344.9 19.0 %collective-permute-done.13 = bf16[1,5,4,4,512]{4,1,3,2,0:T(8,128)(2,1)S(1)} collective-permute-done((bf16[1,5,4,4,512]{4,1,3,2,0:T(8,128)(2,1)S(1)}, bf16[1,5,4,4,512]{4,1,3,2,0:T(8,128)(2,1)S(1)}, u32[]{:S(2)}, u32[]{:S(2)}) %collective-permute-start.13) | collective-permute-done | bytes 81952 | tf_op jit(solution)/shard_map/ppermute | solution.py:20
  364.0 4.4 %conditional.18 = (f32[1,5,4,4,512]{4,1,3,2,0:T(8,128)S(1)}, f32[1,5]{1,0:T(1,128)S(1)}) conditional(s32[]{:T(128)} %convert_element_type.303, f32[1,5,4,4,512]{4,1,3,2,0:T(8,128)S(1)} %convert_select_fusion, (f32[2,4,4,512]{3,2,1,0:T(4,128)S(1)}, s32[]{:T(128)}, f32[1,5,4,4,512]{4,1,3,2,0:T(8,128)S(1)}, bf16[4608,512]{1,0:T(8,128)(2,1)}, ...), branch_computations={%region_24.25_spmd, %region_25.28_spmd} | conditional | flops 378019872 | bytes 8734866 | solution.py:211
  364.5 3.9 subtract_reduce_fusion.3
  369.8 4.7 %collective-permute-done.14 = bf16[1,5,4,4,512]{4,1,3,2,0:T(8,128)(2,1)S(1)} collective-permute-done((bf16[1,5,4,4,512]{4,1,3,2,0:T(8,128)(2,1)S(1)}, bf16[1,5,4,4,512]{4,1,3,2,0:T(8,128)(2,1)S(1)}, u32[]{:S(2)}, u32[]{:S(2)}) %collective-permute-start.14) | collective-permute-done | bytes 81952 | tf_op jit(solution)/shard_map/ppermute | solution.py:20
  374.6 4.4 %conditional.19 = (f32[1,5]{1,0:T(1,128)S(1)}) conditional(s32[]{:T(128)} %convert_element_type.308, () %tuple.122, (f32[5,512]{1,0:T(8,128)S(1)}, pred[1,5,4,4,512]{4,1,3,2,0:T(8,128)(4,1)S(1)}, f32[1,5,4,4,512]{4,1,3,2,0:T(8,128)S(1)}, f32[2,4,4,512]{3,2,1,0:T(4,128)S(1)}, s32[]{:T(128)}, /*index=5*/f32[1,512]{1,0:T(1,128)S(1)}, ...), branch_computations={%region_28.29_spmd, %region_29.32_spmd} | conditional | flops 378104352 | bytes 8693898 | solution.py:211
  375.1 3.9 subtract_reduce_fusion.4
  379.5 13.2 %collective-permute-start.15 = (f32[2,5]{1,0:T(2,128)S(1)}, f32[2,5]{1,0:T(2,128)S(1)}, u32[]{:S(2)}, u32[]{:S(2)}) collective-permute-start(f32[2,5]{1,0:T(2,128)S(1)} %fusion.174), channel_id=1, source_target_pairs={{0,16},{16,0},{32,48},{48,32},{64,80},{80,64},{96,112},{112,96},{1... | collective-permute-start | bytes 128 | tf_op jit(solution)/shard_map/ppermute | solution.py:26
  393.7 6.5 %all_to_all.10 = f32[4,1,5]{2,1,0:T(1,128)S(1)} all-to-all(f32[4,1,5]{2,1,0:T(1,128)S(1)} %bitcast.380), channel_id=1, replica_groups=mesh['segment'=4,'rep'=8,'box'=16] {'segment'}, dimensions={0} | all-to-all | bytes 160 | tf_op jit(solution)/shard_map/all_to_all | solution.py:37
  (225 shorter events, 39.1 us)
Async XLA Ops:
  6.5 39.0 %copy-start = (bf16[512,10]{0,1:T(8,128)(2,1)S(1)}, bf16[512,10]{0,1:T(8,128)(2,1)}, u32[]{:S(2)}) copy-start(bf16[512,10]{0,1:T(8,128)(2,1)} %param.34) | copy-start | bytes 30724
  10.3 16.7 %copy-start.7 = (f32[4,4,4,512]{3,2,1,0:T(4,128)S(1)}, f32[4,4,4,512]{3,2,1,0:T(4,128)}, u32[]{:S(2)}) copy-start(f32[4,4,4,512]{3,2,1,0:T(4,128)} %param.28) | copy-start | bytes 393220
  10.3 16.8 %copy-start.9 = (s32[4]{0:T(128)S(1)}, s32[4]{0:T(128)}, u32[]{:S(2)}) copy-start(s32[4]{0:T(128)} %param.31) | copy-start | bytes 52
  10.3 20.9 %copy-start.8 = (f32[4,4,4,512]{3,2,1,0:T(4,128)S(1)}, f32[4,4,4,512]{3,2,1,0:T(4,128)}, u32[]{:S(2)}) copy-start(f32[4,4,4,512]{3,2,1,0:T(4,128)} %param.29) | copy-start | bytes 393220
  10.3 261.8 %all-to-all-start = ((bf16[16,1,9,32,512]{4,3,2,1,0:T(8,128)(2,1)}), bf16[16,1,9,32,512]{4,3,2,1,0:T(8,128)(2,1)}, u32[]{:S(2)}, u32[]{:S(2)}) async-start(bf16[16,1,9,32,512]{4,3,2,1,0:T(8,128)(2,1)} %stack.2), calls=%async_computation | async-start | bytes 9437184 | tf_op jit(solution)/shard_map/all_to_all | solution.py:10
  26.3 7.2 %copy-start.10 = (s32[4]{0:T(128)S(1)}, s32[4]{0:T(128)}, u32[]{:S(2)}) copy-start(s32[4]{0:T(128)} %param.30) | copy-start | bytes 52
  26.3 18.5 %copy-start.11 = (f32[10]{0:T(128)S(1)}, f32[10]{0:T(128)}, u32[]{:S(2)}) copy-start(f32[10]{0:T(128)} %param.35) | copy-start | bytes 124
  26.3 305.3 %all-gather.2.cloned.1.call-start = ((), (), s32[]{:S(2)}) async-start(), calls=%async_computation.2 | async-start | bytes 5013504 | tf_op jit(solution)/shard_map/all_gather | solution.py:177
  28.3 18.4 %collective-permute-start.1 = (f32[2,8192]{1,0:T(2,128)S(1)}, f32[2,8192]{1,0:T(2,128)S(1)}, u32[]{:S(2)}, u32[]{:S(2)}) collective-permute-start(f32[2,8192]{1,0:T(2,128)S(1)} %fusion.194), channel_id=1, source_target_pairs={{0,16},{16,0},{32,48},{48,32},{64,80},{80,64},{96,112},{112,96},{1... | collective-permute-start | bytes 196616 | tf_op jit(solution)/shard_map/ppermute | solution.py:26
  31.6 15.5 %collective-permute-start.2 = (f32[2,8192]{1,0:T(2,128)S(1)}, f32[2,8192]{1,0:T(2,128)S(1)}, u32[]{:S(2)}, u32[]{:S(2)}) collective-permute-start(f32[2,8192]{1,0:T(2,128)S(1)} %fusion.196), channel_id=1, source_target_pairs={{0,16},{16,0},{32,48},{48,32},{64,80},{80,64},{96,112},{112,96},{1... | collective-permute-start | bytes 196616 | tf_op jit(solution)/shard_map/ppermute | solution.py:26
  33.6 3.8 collective-permute-start
  293.7 2.7 collective-permute-start.4
  295.1 2.1 collective-permute-start.3
  302.1 5.6 %collective-permute-start.6 = (bf16[1,4,4,512]{3,2,1,0:T(4,128)(2,1)S(1)}, bf16[1,4,4,512]{3,2,1,0:T(4,128)(2,1)S(1)}, u32[]{:S(2)}, u32[]{:S(2)}) collective-permute-start(bf16[1,4,4,512]{3,2,1,0:T(4,128)(2,1)S(1)} %convert_element_type.281), channel_id=1, source_target_pairs={{0,128},{128,256},{256,384},{1,129},{129,257},{257,385},{2,130},{1... | collective-permute-start | bytes 49160 | tf_op jit(solution)/shard_map/ppermute | solution.py:20
  305.8 2.8 collective-permute-start.5
  308.7 10.5 %collective-permute-start.8 = (bf16[1,4,4,512]{3,2,1,0:T(4,128)(2,1)S(1)}, bf16[1,4,4,512]{3,2,1,0:T(4,128)(2,1)S(1)}, u32[]{:S(2)}, u32[]{:S(2)}) collective-permute-start(bf16[1,4,4,512]{3,2,1,0:T(4,128)(2,1)S(1)} %convert_element_type.286), channel_id=1, source_target_pairs={{0,128},{128,256},{256,384},{1,129},{129,257},{257,385},{2,130},{1... | collective-permute-start | bytes 49160 | tf_op jit(solution)/shard_map/ppermute | solution.py:20
  317.2 2.8 collective-permute-start.7
  320.2 10.5 %collective-permute-start.10 = (bf16[1,4,4,512]{3,2,1,0:T(4,128)(2,1)S(1)}, bf16[1,4,4,512]{3,2,1,0:T(4,128)(2,1)S(1)}, u32[]{:S(2)}, u32[]{:S(2)}) collective-permute-start(bf16[1,4,4,512]{3,2,1,0:T(4,128)(2,1)S(1)} %convert_element_type.291), channel_id=1, source_target_pairs={{0,128},{128,256},{256,384},{1,129},{129,257},{257,385},{2,130},{1... | collective-permute-start | bytes 49160 | tf_op jit(solution)/shard_map/ppermute | solution.py:20
  323.9 7.6 %collective-permute-start.9 = (bf16[1,4,4,512]{3,2,1,0:T(4,128)(2,1)S(1)}, bf16[1,4,4,512]{3,2,1,0:T(4,128)(2,1)S(1)}, u32[]{:S(2)}, u32[]{:S(2)}) collective-permute-start(bf16[1,4,4,512]{3,2,1,0:T(4,128)(2,1)S(1)} %convert_element_type.289), channel_id=1, source_target_pairs={{0,128},{128,256},{256,384},{1,129},{129,257},{257,385},{2,130},{1... | collective-permute-start | bytes 49160 | tf_op jit(solution)/shard_map/ppermute | solution.py:20
  331.7 6.0 %collective-permute-start.11 = (bf16[1,5,4,4,512]{4,1,3,2,0:T(8,128)(2,1)S(1)}, bf16[1,5,4,4,512]{4,1,3,2,0:T(8,128)(2,1)S(1)}, u32[]{:S(2)}, u32[]{:S(2)}) collective-permute-start(bf16[1,5,4,4,512]{4,1,3,2,0:T(8,128)(2,1)S(1)} %convert_element_type.296), channel_id=1, source_target_pairs={{128,0},{256,128},{384,256},{129,1},{257,129},{385,257},{130,2},{2... | collective-permute-start | bytes 245768 | tf_op jit(solution)/shard_map/ppermute | solution.py:20
  337.8 5.7 %collective-permute-start.12 = (bf16[1,5,4,4,512]{4,1,3,2,0:T(8,128)(2,1)S(1)}, bf16[1,5,4,4,512]{4,1,3,2,0:T(8,128)(2,1)S(1)}, u32[]{:S(2)}, u32[]{:S(2)}) collective-permute-start(bf16[1,5,4,4,512]{4,1,3,2,0:T(8,128)(2,1)S(1)} %convert_element_type.301), channel_id=1, source_target_pairs={{128,0},{256,128},{384,256},{129,1},{257,129},{385,257},{130,2},{2... | collective-permute-start | bytes 245768 | tf_op jit(solution)/shard_map/ppermute | solution.py:20
  343.6 20.4 %collective-permute-start.13 = (bf16[1,5,4,4,512]{4,1,3,2,0:T(8,128)(2,1)S(1)}, bf16[1,5,4,4,512]{4,1,3,2,0:T(8,128)(2,1)S(1)}, u32[]{:S(2)}, u32[]{:S(2)}) collective-permute-start(bf16[1,5,4,4,512]{4,1,3,2,0:T(8,128)(2,1)S(1)} %convert_element_type.306), channel_id=1, source_target_pairs={{128,0},{256,128},{384,256},{129,1},{257,129},{385,257},{130,2},{2... | collective-permute-start | bytes 245768 | tf_op jit(solution)/shard_map/ppermute | solution.py:20
  368.5 6.1 %collective-permute-start.14 = (bf16[1,5,4,4,512]{4,1,3,2,0:T(8,128)(2,1)S(1)}, bf16[1,5,4,4,512]{4,1,3,2,0:T(8,128)(2,1)S(1)}, u32[]{:S(2)}, u32[]{:S(2)}) collective-permute-start(bf16[1,5,4,4,512]{4,1,3,2,0:T(8,128)(2,1)S(1)} %convert_element_type.311), channel_id=1, source_target_pairs={{128,0},{256,128},{384,256},{129,1},{257,129},{385,257},{130,2},{2... | collective-permute-start | bytes 245768 | tf_op jit(solution)/shard_map/ppermute | solution.py:20
  379.5 14.0 %collective-permute-start.15 = (f32[2,5]{1,0:T(2,128)S(1)}, f32[2,5]{1,0:T(2,128)S(1)}, u32[]{:S(2)}, u32[]{:S(2)}) collective-permute-start(f32[2,5]{1,0:T(2,128)S(1)} %fusion.174), channel_id=1, source_target_pairs={{0,16},{16,0},{32,48},{48,32},{64,80},{80,64},{96,112},{112,96},{1... | collective-permute-start | bytes 128 | tf_op jit(solution)/shard_map/ppermute | solution.py:26
  (3 other events, 14.0 us)
Sparse Core Ops, SparseCore 0:
  29.2 251.3 all-gather.1
